TPU v7x, 32 devices: a whole 2x2x4 slice. The times are simulated.
32 devices in a mesh: rows: 8 (over z, y), grp: 4 (over x, core).
Axes of the slice: x: 2, y: 2, z: 4, core: 2. Of those that a mesh axis runs over, the one named last changes fastest.
Arguments:
- mat: float32 [16384, 1024], P(('rows', 'grp'))
- signs: int32 [16384], P(('rows', 'grp')), may hold values from -1 to 1, as said below
- picks: int32 [2048], P(('rows', 'grp')), may hold values from 0 to 16383, as said below
- rhs: float32 [16384, 128], P(('rows', 'grp'))
Outputs:
- tri: float32 [1024, 1024], replicated
- solution: float32 [1024, 128], replicated
- residual: float32 [16384, 128], P(('rows', 'grp'))
Inputs may be any that keep to these rules, and one draw needn't show every extreme that they name: `signs`: every entry is -1 or 1. `picks`: the entries k * 64 to (k + 1) * 64 - 1 are distinct row indices in k * 512 to (k + 1) * 512 - 1.
All inputs are finite; a program needn't handle non-finite values.
Results may differ from a plain program's by a relative error of at most 0.000088.
Values sent between devices are 32-bit elements; how exact they have to be, the bound alone decides.
A program may use at most 64 MiB of HBM per device.

v0:
```python
import math

import jax
import jax.numpy as jnp
from jax import lax
from jax.sharding import PartitionSpec as P

exact_mode = lax.Precision.HIGHEST


def partner_2(block, axis, apart):
    count = lax.axis_size(axis)
    route = []
    for low in range(count):
        high = low | 1 << apart
        if high != low and high < count:
            route += [(low, high), (high, low)]
    return lax.ppermute(block, axis, route)


def walsh_table(table_order):
    counter = lax.iota(jnp.int32, table_order)
    common_bits = counter[:, None] & counter[None, :]
    parity = jnp.zeros((table_order, table_order), jnp.int32)
    for bit_pos in range(max(table_order.bit_length() - 1, 0)):
        parity = parity + (common_bits >> bit_pos & 1)
    return jnp.where(parity % 2 == 0, 1.0, -1.0).astype(jnp.float32)


def local_mix(block):
    row_count, col_count = block.shape
    first = 1 << row_count.bit_length() // 2
    second = row_count // first
    cube = block.reshape(first, second, col_count)
    cube = jnp.einsum("ia,abn->ibn", walsh_table(first), cube, precision=exact_mode)
    cube = jnp.einsum("jb,ibn->ijn", walsh_table(second), cube, precision=exact_mode)
    return cube.reshape(row_count, col_count)


def shards(mat, signs, picks, rhs):
    row_count, col_count = mat.shape
    rows_size = lax.axis_size("rows")
    grp_size = lax.axis_size("grp")
    samples = picks.shape[0] * rows_size * grp_size
    mixed = mat * (signs.astype(jnp.float32) * (1.0 / math.sqrt(samples)))[:, None]
    mixed = local_mix(mixed)
    for bit_pos in range(grp_size.bit_length() - 1):
        partner = partner_2(mixed, "grp", bit_pos)
        upper_side = lax.axis_index("grp") >> bit_pos & 1
        mixed = jnp.where(upper_side == 1, partner - mixed, mixed + partner)
    piece = row_count // rows_size
    turned = lax.all_to_all(mixed, "rows", split_axis=0, concat_axis=0, tiled=True).reshape(
        rows_size, piece, col_count
    )
    turned = jnp.einsum("rs,slc->rlc", walsh_table(rows_size), turned, precision=exact_mode)
    every_pick = (
        lax.all_gather(picks, "rows", axis=0, tiled=True).reshape(rows_size, -1) % row_count
    )
    local_pos = lax.axis_index("rows") * piece + lax.iota(jnp.int32, piece)
    hits = jnp.sum((every_pick[:, :, None] == local_pos[None, None, :]).astype(jnp.float32), axis=1)
    weighted = (turned * hits[:, :, None]).reshape(row_count, col_count)
    gram_part = jnp.dot(weighted.T, turned.reshape(row_count, col_count), precision=exact_mode)
    squares_part = jnp.sum(rhs * rhs, axis=0)
    atb_part = jnp.dot(mat.T, rhs, precision=exact_mode)
    squares_all, atb = lax.psum((squares_part, atb_part), ("rows", "grp"))
    gram = lax.psum(gram_part, ("rows", "grp"))
    lower = jnp.linalg.cholesky(gram)
    beta = jnp.sqrt(squares_all)
    lifted = lax.linalg.triangular_solve(lower, atb, left_side=True, lower=True) / beta
    alpha = jnp.sqrt(jnp.sum(lifted * lifted, axis=0))
    unit = lifted / alpha
    direction = lax.linalg.triangular_solve(
        lower, unit, left_side=True, lower=True, transpose_a=True
    )
    image = jnp.dot(mat, direction, precision=exact_mode)
    pushed = image - alpha / beta * rhs
    gamma_sq = lax.psum(jnp.sum(pushed * pushed, axis=0), ("rows", "grp"))
    gamma = jnp.sqrt(gamma_sq)
    coef = beta * alpha / (alpha * alpha + gamma * gamma)
    return (lower.T, direction * coef, rhs - image * coef)


def solution(mesh):
    return jax.shard_map(
        shards,
        mesh=mesh,
        in_specs=(
            P(("rows", "grp"), None),
            P(("rows", "grp")),
            P(("rows", "grp")),
            P(("rows", "grp"), None),
        ),
        out_specs=(P(), P(), P(("rows", "grp"), None)),
        check_vma=False,
    )
```

profile of v0, /device:TPU:0, one launch (start us, length us, event | category | flops | bytes accessed | tf_op | source)
XLA Modules:
  0.0 695.5 jit_solution(4220823933039098707)
XLA Ops:
  9.6 3.0 fusion.12
  12.6 3.2 fusion.10
  16.5 3.9 collective-permute-done
  20.4 3.4 add_select_fusion.1
  23.8 2.9 collective-permute-start.1
  26.6 46.2 %collective-permute-done.1 = f32[512,1024]{1,0:T(8,128)} collective-permute-done((f32[512,1024]{1,0:T(8,128)}, f32[512,1024]{1,0:T(8,128)}, u32[]{:S(2)}, u32[]{:S(2)}) %collective-permute-start.1) | collective-permute-done | bytes 2097184 | tf_op jit(solution)/shard_map/ppermute | solution.py:18
  72.9 4.2 add_select_fusion
  77.1 6.1 all-to-all-start
  84.7 46.8 %all-reduce.1 = s32[512]{0:T(512)S(1)} all-reduce(s32[512]{0:T(512)S(1)} %dynamic-update-slice.47), channel_id=1, replica_groups=mesh['rows'=8,'grp'=4] {'rows'}, use_global_device_ids=true, to_apply=%add.1 | all-reduce | flops 512 | bytes 4096
  131.8 4.2 fusion.170
  136.1 4.5 fusion.8
  140.6 8.9 %fusion.5 = f32[1024,1024]{0,1:T(8,128)} fusion(f32[8,64,1024]{2,0,1:T(8,128)S(1)} %fusion.8, f32[8,64]{0,1:T(8,128)S(1)} %copy.36), kind=kOutput, calls=%fused_computation.10 | convolution fusion | flops 6442975232 | bytes 6293504 | tf_op jit(solution)/shard_map/dot_general | solution.py:62
  149.7 38.4 %psum.30 = f32[128]{0:T(128)S(1)} all-reduce(f32[128]{0:T(128)S(1)} %multiply_reduce_fusion.2), channel_id=1, replica_groups=mesh['rows'=8,'grp'=4] {'rows','grp'}, use_global_device_ids=true, to_apply=%region_20.21 | all-reduce | flops 128 | bytes 1024 | tf_op jit(solution)/shard_map/psum | solution.py:65
  188.1 106.0 %all-reduce.5.cloned.1.call-done = (f32[1024,1024]{0,1:T(8,128)}, f32[1024,128]{1,0:T(8,128)}) async-done(((f32[1024,1024]{0,1:T(8,128)}, f32[1024,128]{1,0:T(8,128)}), (f32[1024,1024]{0,1:T(8,128)}, f32[1024,128]{1,0:T(8,128)})) %all-reduce.5.cloned.1.call-update) | async-done | bytes 4718608 | tf_op jit(solution)/shard_map/psum | solution.py:66
  294.2 5.5 copy.38
  299.6 4.4 fusion
  306.0 11.7 %cholesky.223 = f32[128,128]{1,0:T(8,128)S(1)} custom-call(f32[128,128]{1,0:T(8,128)S(1)} %cholesky.580), custom_call_target="Cholesky" | custom-call | tf_op jit(solution)/shard_map/jit(cholesky)/cholesky | solution.py:67
  317.8 9.8 %custom-call.64 = f32[1,128,128]{1,2,0:T(8,128)S(1)} custom-call(f32[1,128,128]{2,1,0:T(8,128)S(1)} %get-tuple-element.83), custom_call_target="InvertDiagBlocksLowerTriangular" | custom-call | tf_op jit(solution)/shard_map/jit(cholesky)/cholesky | solution.py:67
  327.6 2.5 cholesky.255
  330.1 2.3 constant_dynamic-update-slice_fusion.56
  334.0 11.9 %cholesky.244 = f32[128,128]{1,0:T(8,128)S(1)} custom-call(f32[128,128]{1,0:T(8,128)S(1)} %cholesky.584), custom_call_target="Cholesky" | custom-call | tf_op jit(solution)/shard_map/jit(cholesky)/cholesky | solution.py:67
  346.5 9.8 %custom-call.65 = f32[1,128,128]{1,2,0:T(8,128)S(1)} custom-call(f32[1,128,128]{2,1,0:T(8,128)S(1)} %get-tuple-element.80), custom_call_target="InvertDiagBlocksLowerTriangular" | custom-call | tf_op jit(solution)/shard_map/jit(cholesky)/cholesky | solution.py:67
  359.7 11.7 %cholesky.468 = f32[128,128]{1,0:T(8,128)S(1)} custom-call(f32[128,128]{1,0:T(8,128)S(1)} %cholesky.589), custom_call_target="Cholesky" | custom-call | tf_op jit(solution)/shard_map/jit(cholesky)/cholesky | solution.py:67
  372.7 9.8 %custom-call.66 = f32[1,128,128]{1,2,0:T(8,128)S(1)} custom-call(f32[1,128,128]{2,1,0:T(8,128)S(1)} %get-tuple-element.77), custom_call_target="InvertDiagBlocksLowerTriangular" | custom-call | tf_op jit(solution)/shard_map/jit(cholesky)/cholesky | solution.py:67
  383.6 2.3 convolution_subtract_fusion.2
  386.0 12.1 %cholesky.487 = f32[128,128]{1,0:T(8,128)S(1)} custom-call(f32[128,128]{1,0:T(8,128)S(1)} %cholesky.594), custom_call_target="Cholesky" | custom-call | tf_op jit(solution)/shard_map/jit(cholesky)/cholesky | solution.py:67
  399.4 9.8 %custom-call.67 = f32[1,128,128]{1,2,0:T(8,128)S(1)} custom-call(f32[1,128,128]{2,1,0:T(8,128)S(1)} %get-tuple-element.74), custom_call_target="InvertDiagBlocksLowerTriangular" | custom-call | tf_op jit(solution)/shard_map/jit(cholesky)/cholesky | solution.py:67
  410.3 2.3 convolution_subtract_fusion.3
  412.7 11.7 %cholesky.506 = f32[128,128]{1,0:T(8,128)S(1)} custom-call(f32[128,128]{1,0:T(8,128)S(1)} %cholesky.599), custom_call_target="Cholesky" | custom-call | tf_op jit(solution)/shard_map/jit(cholesky)/cholesky | solution.py:67
  425.7 10.0 %custom-call.68 = f32[1,128,128]{1,2,0:T(8,128)S(1)} custom-call(f32[1,128,128]{2,1,0:T(8,128)S(1)} %get-tuple-element.71), custom_call_target="InvertDiagBlocksLowerTriangular" | custom-call | tf_op jit(solution)/shard_map/jit(cholesky)/cholesky | solution.py:67
  439.0 11.7 %cholesky.526 = f32[128,128]{1,0:T(8,128)S(1)} custom-call(f32[128,128]{1,0:T(8,128)S(1)} %cholesky.604), custom_call_target="Cholesky" | custom-call | tf_op jit(solution)/shard_map/jit(cholesky)/cholesky | solution.py:67
  452.0 9.8 %custom-call.69 = f32[1,128,128]{1,2,0:T(8,128)S(1)} custom-call(f32[1,128,128]{2,1,0:T(8,128)S(1)} %get-tuple-element.68), custom_call_target="InvertDiagBlocksLowerTriangular" | custom-call | tf_op jit(solution)/shard_map/jit(cholesky)/cholesky | solution.py:67
  464.8 11.9 %cholesky.546 = f32[128,128]{1,0:T(8,128)S(1)} custom-call(f32[128,128]{1,0:T(8,128)S(1)} %cholesky.609), custom_call_target="Cholesky" | custom-call | tf_op jit(solution)/shard_map/jit(cholesky)/cholesky | solution.py:67
  478.0 9.8 %custom-call.70 = f32[1,128,128]{1,2,0:T(8,128)S(1)} custom-call(f32[1,128,128]{2,1,0:T(8,128)S(1)} %get-tuple-element.65), custom_call_target="InvertDiagBlocksLowerTriangular" | custom-call | tf_op jit(solution)/shard_map/jit(cholesky)/cholesky | solution.py:67
  490.4 11.7 %cholesky.564 = f32[128,128]{1,0:T(8,128)S(1)} custom-call(f32[128,128]{1,0:T(8,128)S(1)} %convolution_subtract_fusion.16), custom_call_target="Cholesky" | custom-call | tf_op jit(solution)/shard_map/jit(cholesky)/cholesky | solution.py:67
  509.1 6.8 fusion.1
  516.0 28.1 %while.1 = (s32[]{:T(128)}, f32[1024,1024]{1,0:T(8,128)}, s32[8,2]{0,1:T(2,128)S(1)}, f32[8,128,128]{2,1,0:T(8,128)}, s32[]{:T(128)}) while((s32[]{:T(128)}, f32[1024,1024]{1,0:T(8,128)}, s32[8,2]{0,1:T(2,128)S(1)}, f32[8,128,128]{2,1,0:T(8,128)}, s32[]{:T(128)}) %tuple.71), condition=%wide.while_cond, body=%wide.while_body.sunk | while | flops 2 | bytes 132705 | solution.py:72
  516.6 2.9 bitcast_dynamic-update-slice_fusion.2
  520.1 2.9 bitcast_dynamic-update-slice_fusion.2
  523.6 2.9 bitcast_dynamic-update-slice_fusion.2
  527.2 2.9 bitcast_dynamic-update-slice_fusion.2
  530.7 2.9 bitcast_dynamic-update-slice_fusion.2
  534.2 2.9 bitcast_dynamic-update-slice_fusion.2
  537.7 2.9 bitcast_dynamic-update-slice_fusion.2
  541.2 2.8 bitcast_dynamic-update-slice_fusion.2
  544.1 79.6 %custom-call.71 = f32[8,128,128]{1,2,0:T(8,128)S(1)} custom-call(f32[8,128,128]{2,1,0:T(8,128)} %get-tuple-element.10), custom_call_target="InvertDiagBlocksLowerTriangular" | custom-call | tf_op jit(solution)/shard_map/triangular_solve | solution.py:72
  642.1 39.0 %psum.31 = f32[128]{0:T(128)S(1)} all-reduce(f32[128]{0:T(128)S(1)} %get-tuple-element.98), channel_id=1, replica_groups=mesh['rows'=8,'grp'=4] {'rows','grp'}, use_global_device_ids=true, to_apply=%region_23.24 | all-reduce | flops 128 | bytes 1024 | tf_op jit(solution)/shard_map/psum | solution.py:77
  682.9 5.3 copy.41
  (143 shorter events, 56.2 us)
Async XLA Ops:
  15.9 4.5 collective-permute-start
  23.8 49.1 %collective-permute-start.1 = (f32[512,1024]{1,0:T(8,128)}, f32[512,1024]{1,0:T(8,128)}, u32[]{:S(2)}, u32[]{:S(2)}) collective-permute-start(f32[512,1024]{1,0:T(8,128)} %add_select_fusion.1), channel_id=1, source_target_pairs={{0,2},{2,0},{1,3},{3,1},{4,6},{6,4},{5,7},{7,5},{8,10},{10,8},{9,1... | collective-permute-start | bytes 6291464 | tf_op jit(solution)/shard_map/ppermute | solution.py:18
  26.6 56.6 %copy-start.6 = (u32[32]{0:T(128)S(1)}, u32[32]{0:T(128)}, u32[]{:S(2)}) copy-start(u32[32]{0:T(128)} %constant.376) | copy-start | bytes 388
  26.6 57.8 %copy-start.5 = (s32[64]{0:T(128)S(1)}, s32[64]{0:T(128)}, u32[]{:S(2)}) copy-start(s32[64]{0:T(128)} %param.6) | copy-start | bytes 772
  26.6 105.2 %copy-start = (f32[512,1024]{1,0:T(8,128)S(1)}, f32[512,1024]{1,0:T(8,128)}, u32[]{:S(2)}) copy-start(f32[512,1024]{1,0:T(8,128)} %param.4) | copy-start | bytes 6291460
  26.6 105.2 %copy-start.3 = (f32[512,128]{1,0:T(8,128)S(1)}, f32[512,128]{1,0:T(8,128)}, u32[]{:S(2)}) copy-start(f32[512,128]{1,0:T(8,128)} %param.7) | copy-start | bytes 786436
  77.1 59.0 %all-to-all-start = ((f32[8,64,1024]{2,1,0:T(8,128)}), f32[8,64,1024]{2,1,0:T(8,128)}, u32[]{:S(2)}, u32[]{:S(2)}) async-start(f32[8,64,1024]{2,1,0:T(8,128)} %bitcast.153), calls=%async_computation | async-start | bytes 4194304 | tf_op jit(solution)/shard_map/all_to_all | solution.py:52
  83.1 211.0 %all-reduce.5.cloned.1.call-start = ((), (), s32[]{:S(2)}) async-start(), calls=%async_computation.1 | async-start | bytes 9437184 | tf_op jit(solution)/shard_map/psum | solution.py:66
  304.1 1.9 copy-start.2
  509.1 114.6 %copy-start.4 = (f32[1024,128]{1,0:T(8,128)S(1)}, f32[1024,128]{1,0:T(8,128)}, u32[]{:S(2)}) copy-start(f32[1024,128]{1,0:T(8,128)} %get-tuple-element.32) | copy-start | bytes 1572868
  623.7 8.2 %copy-start.1 = (f32[1024,1024]{1,0:T(8,128)S(1)}, f32[1024,1024]{1,0:T(8,128)}, u32[]{:S(2)}) copy-start(f32[1024,1024]{1,0:T(8,128)} %get-tuple-element.152) | copy-start | bytes 12582916
Sparse Core Ops, SparseCore 0:
  149.6 144.4 all-reduce.4
where the time goes:
time: 703 us; the launch traced here: 695 us
  other arithmetic  275 us (39%)
  waiting for transfers between devices  156 us (22%)
  blocking collectives  124 us (18%)
  matrix products  64.3 us (9%)
  local copies, waits for them, and re-layouts  45.5 us (6%)
  between operations  20.9 us (3%)
  starting transfers between devices  9.53 us (1%)
    another operation x30, other arithmetic, shards(): lower = jnp.linalg.cholesky(gram)  172 us
    psum x1, waiting for transfers between devices, shards(): gram = lax.psum(gram_part, ('rows', 'grp'))  106 us
    another operation x3, other arithmetic, shards(): lax.linalg.triangular_solve(lower, unit, left_side=True, lower=True, tran...  86.5 us
    ppermute x2, waiting for transfers between devices, partner_2(): return lax.ppermute(block, axis, route)  50.1 us
    unnamed x1, blocking collectives  46.8 us
    psum x1, blocking collectives, shards(): gamma_sq = lax.psum(jnp.sum(pushed * pushed, axis=0), ('rows', 'grp'))  39 us
    psum x1, blocking collectives, shards(): squares_all, atb = lax.psum((squares_part, atb_part), ('rows', 'grp'))  38.4 us
    another operation x24, local copies, waits for them, and re-layouts  28 us
  transfers between devices with their start and end apart: 4, of which 3 were waited for; matrix products, arithmetic and copies ran while one was open for 1% of the time, Pallas kernels for 0%

commit v1 on v0

v1 whole, which is shorter than its diff:
```python
import functools

import jax
import jax.numpy as jnp
from jax import lax
from jax.experimental import pallas as pl
from jax.experimental.pallas import tpu as pltpu
from jax.sharding import PartitionSpec as P

exact_mode = lax.Precision.HIGHEST
TILE = 128
SUB = 8
AXES = ("rows", "grp")


def walsh_table(table_order, piece=1):
    counter = lax.iota(jnp.int32, table_order)
    outer = counter // piece
    common_bits = outer[:, None] & outer[None, :]
    parity = jnp.zeros((table_order, table_order), jnp.int32)
    for bit_pos in range(max((table_order // piece).bit_length() - 1, 0)):
        parity = parity + (common_bits >> bit_pos & 1)
    table = jnp.where(parity % 2 == 0, 1.0, -1.0).astype(jnp.float32)
    inner = counter % piece
    return jnp.where(inner[:, None] == inner[None, :], table, 0.0)


def dot_tt(a, b):
    return lax.dot_general(a, b, (((0,), (0,)), ((), ())), precision=exact_mode,
                           preferred_element_type=jnp.float32)


def dot_nn(a, b):
    return lax.dot_general(a, b, (((1,), (0,)), ((), ())), precision=exact_mode,
                           preferred_element_type=jnp.float32)


def factor_tile(block):
    groups = TILE // SUB
    lane = lax.broadcasted_iota(jnp.int32, (SUB, TILE), 1)
    sub = lax.broadcasted_iota(jnp.int32, (SUB, TILE), 0)
    left = [block[SUB * g:SUB * (g + 1), :] for g in range(groups)]
    right = [(lane == sub + SUB * g).astype(jnp.float32) for g in range(groups)]
    for j in range(TILE):
        g, s = divmod(j, SUB)
        inv = 1.0 / left[g][s:s + 1, j:j + 1]
        row = left[g][s:s + 1, :] * inv
        row_e = right[g][s:s + 1, :] * inv
        for h in range(g, groups):
            col = jnp.broadcast_to(left[h][:, j:j + 1], (SUB, TILE))
            if h == g:
                if s == SUB - 1:
                    continue
                col = jnp.where(sub > s, col, 0.0)
            left[h] = left[h] - col * row
            right[h] = right[h] - col * row_e
    for g in range(groups):
        pivot = jnp.sum(jnp.where(lane == sub + SUB * g, left[g], 0.0), axis=1, keepdims=True)
        root = jnp.sqrt(pivot)
        left[g] = jnp.where(lane >= sub + SUB * g, left[g] / root, 0.0)
        right[g] = jnp.where(lane <= sub + SUB * g, right[g] / root, 0.0)
    return jnp.concatenate(left, axis=0), jnp.concatenate(right, axis=0)


def factor_kernel(packed_ref, atb_ref, squares_ref, tri_ref, direction_ref, alpha_ref, work, inverse):
    n = tri_ref.shape[0]
    tiles = n // TILE
    offset = 0
    for i in range(tiles):
        width = n - i * TILE
        work[i * TILE:(i + 1) * TILE, i * TILE:n] = packed_ref[:, offset:offset + width]
        if i:
            work[i * TILE:(i + 1) * TILE, :i * TILE] = jnp.zeros((TILE, i * TILE), jnp.float32)
        offset += width
    work[:, n:] = atb_ref[...]
    width = work.shape[1]

    def step(k, carry):
        at = pl.multiple_of(k * TILE, TILE)
        here = pl.ds(at, TILE)
        upper, inv = factor_tile(work[here, here])
        inverse[here, :] = inv
        column = lax.broadcasted_iota(jnp.int32, (TILE, width), 1)
        panel = dot_nn(inv, work[here, :])
        work[here, :] = jnp.where(column >= at + TILE, panel, 0.0)
        work[here, here] = upper

        def trail(i, carry):
            there = pl.ds(pl.multiple_of(i * TILE, TILE), TILE)
            work[there, :] = work[there, :] - dot_tt(work[here, there], work[here, :])
            return carry

        return lax.fori_loop(k + 1, tiles, trail, carry)

    lax.fori_loop(0, tiles, step, 0)
    tri_ref[...] = work[:, :n]
    beta = jnp.sqrt(squares_ref[0:1, :])
    lifted = work[:, n:] / beta
    alpha = jnp.sqrt(jnp.sum(lifted * lifted, axis=0, keepdims=True))
    alpha_ref[...] = jnp.broadcast_to(alpha, alpha_ref.shape)
    work[:, n:] = lifted / alpha
    direction_ref[...] = jnp.zeros_like(direction_ref)

    def back(t, carry):
        k = tiles - 1 - t
        here = pl.ds(pl.multiple_of(k * TILE, TILE), TILE)
        rest = work[here, n:] - dot_nn(tri_ref[here, :], direction_ref[...])
        direction_ref[here, :] = dot_tt(inverse[here, :], rest)
        return carry

    lax.fori_loop(0, tiles, back, 0)


def factor_and_solve(packed, atb, squares):
    n, k = atb.shape
    return pl.pallas_call(
        factor_kernel,
        out_shape=(
            jax.ShapeDtypeStruct((n, n), jnp.float32),
            jax.ShapeDtypeStruct((n, k), jnp.float32),
            jax.ShapeDtypeStruct((SUB, k), jnp.float32),
        ),
        in_specs=[pl.BlockSpec(memory_space=pltpu.VMEM)] * 3,
        out_specs=(pl.BlockSpec(memory_space=pltpu.VMEM),) * 3,
        scratch_shapes=[
            pltpu.VMEM((n, n + k), jnp.float32),
            pltpu.VMEM((n, TILE), jnp.float32),
        ],
        compiler_params=pltpu.CompilerParams(vmem_limit_bytes=48 * 1024 * 1024),
        name="factor_and_solve",
    )(packed, atb, squares)


def shards(mat, signs, picks, rhs):
    row_count, n = mat.shape
    devices = lax.axis_size("rows") * lax.axis_size("grp")
    samples = picks.shape[0] * devices
    piece = row_count // devices

    atb_part = dot_tt(mat, rhs)
    squares_part = jnp.sum(rhs * rhs, axis=0, keepdims=True)
    squares_part = jnp.concatenate(
        [squares_part, jnp.zeros((SUB - 1, rhs.shape[1]), jnp.float32)], axis=0
    )
    early = lax.psum(jnp.concatenate([atb_part, squares_part], axis=0), AXES)
    atb, squares = early[:n], early[n:]

    local_rows = lax.iota(jnp.int32, row_count)
    hits = jnp.sum(
        ((picks % row_count)[:, None] == local_rows[None, :]).astype(jnp.float32), axis=0
    ) * (1.0 / samples)
    hits = lax.all_to_all(hits.reshape(devices, piece), AXES, 0, 0, tiled=True)

    mixed = mat * signs.astype(jnp.float32)[:, None]
    mixed = dot_nn(walsh_table(row_count), mixed)
    if piece % SUB == 0:
        turned = lax.all_to_all(mixed, AXES, 0, 0, tiled=True)
    else:
        turned = mixed.reshape(devices, piece * n // TILE, TILE)
        turned = lax.all_to_all(turned, AXES, 0, 0, tiled=True).reshape(row_count, n)
    turned = dot_nn(walsh_table(row_count, piece), turned)
    weighted = turned * hits.reshape(row_count, 1)
    strips = [
        dot_tt(weighted[:, at:at + TILE], turned[:, at:]) for at in range(0, n, TILE)
    ]
    packed = lax.psum(jnp.concatenate(strips, axis=1), AXES)

    tri, direction, alpha = factor_and_solve(packed, atb, squares)
    alpha = alpha[0]
    beta = jnp.sqrt(squares[0])
    image = dot_nn(mat, direction)
    pushed = image - alpha / beta * rhs
    gamma_sq = lax.psum(jnp.sum(pushed * pushed, axis=0), AXES)
    coef = beta * alpha / (alpha * alpha + gamma_sq)
    return (tri, direction * coef, rhs - image * coef)


def solution(mesh):
    return jax.shard_map(
        shards,
        mesh=mesh,
        in_specs=(P(AXES, None), P(AXES), P(AXES), P(AXES, None)),
        out_specs=(P(), P(), P(AXES, None)),
        check_vma=False,
    )
```

time: 703 us -> 410 us (0.58)
  other arithmetic: 275 us -> 4.5 us
  Pallas kernels: 0 us -> 119 us
  blocking collectives: 124 us -> 40 us
  local copies, waits for them, and re-layouts: 45.5 us -> 7.34 us
  matrix products: 64.3 us -> 32.4 us
  waiting for transfers between devices: 156 us -> 179 us
    another operation x33 -> x0, other arithmetic: 259 us -> none  [the longest x30 172 us: shards(): lower = jnp.linalg.cholesky(gram)]
    pallas_call x0 -> x1, Pallas kernels: none -> 119 us  [factor_and_solve(): pl.pallas_call(factor_kernel, out_shape=(jax.ShapeDtypeStruct((n, n), jnp...]
    ppermute x2 -> x0, waiting for transfers between devices: 50.1 us -> none  [partner_2(): return lax.ppermute(block, axis, route)]
    unnamed x1 -> x0, blocking collectives: 46.8 us -> none
    all_to_all x1 -> x2, waiting for transfers between devices: 0.01 us -> 42.2 us  [the longest x1 42.2 us: shards(): turned = lax.all_to_all(mixed, AXES, 0, 0, tiled=True)]
    another operation x44 -> x0, matrix products: 38.5 us -> none  [the longest x14 22.9 us: shards(): lower = jnp.linalg.cholesky(gram)]
    psum x2 -> x1, blocking collectives: 77.4 us -> 40 us  [shards(): gamma_sq = lax.psum(jnp.sum(pushed * pushed, axis=0), AXES)]
    another operation x37 -> x0, local copies, waits for them, and re-layouts: 30.7 us -> none
  transfers between devices with their start and end apart: 4 -> 3, of which waited for: 3 -> 2; matrix products, arithmetic and copies ran while one was open for 1% -> 4% of each run, Pallas kernels for 0% -> 0%
where the time goes in v1:
time: 410 us; the launch traced here: 409 us
  waiting for transfers between devices  179 us (44%)
  Pallas kernels  119 us (29%)
  blocking collectives  40 us (10%)
  matrix products  32.4 us (8%)
  between operations  14.1 us (3%)
  starting transfers between devices  13.3 us (3%)
  local copies, waits for them, and re-layouts  7.34 us (2%)
  other arithmetic  4.5 us (1%)
    psum x1, waiting for transfers between devices, shards(): packed = lax.psum(jnp.concatenate(strips, axis=1), AXES)  137 us
    pallas_call x1, Pallas kernels, factor_and_solve(): pl.pallas_call(factor_kernel, out_shape=(jax.ShapeDtypeStruct((n, n), jnp...  119 us
    all_to_all x1, waiting for transfers between devices, shards(): turned = lax.all_to_all(mixed, AXES, 0, 0, tiled=True)  42.2 us
    psum x1, blocking collectives, shards(): gamma_sq = lax.psum(jnp.sum(pushed * pushed, axis=0), AXES)  40 us
    dot_general x9, matrix products, dot_tt(): lax.dot_general(a, b, (((0,), (0,)), ((), ())), precision=exact_mode, pre...  16.5 us
    dot_general x3, matrix products, dot_nn(): lax.dot_general(a, b, (((1,), (0,)), ((), ())), precision=exact_mode, pre...  15.9 us
  transfers between devices with their start and end apart: 3, of which 2 were waited for; matrix products, arithmetic and copies ran while one was open for 4% of the time, Pallas kernels for 0%

profile of v1, /device:TPU:0, one launch (start us, length us, event | category | flops | bytes accessed | tf_op | source)
XLA Modules:
  0.0 409.4 jit_solution(14978225188838205383)
XLA Ops:
  7.2 0.7 and_select_fusion
  7.8 0.1 convert_reduce_fusion
  7.9 0.7 mul.83
  8.6 7.3 %all-to-all-start.1 = ((f32[32,1,16]{2,1,0:T(1,128)}), f32[32,1,16]{2,1,0:T(1,128)S(1)}, u32[]{:S(2)}, u32[]{:S(2)}) async-start(f32[32,1,16]{2,1,0:T(1,128)} %bitcast.2), calls=%async_computation.1 | async-start | bytes 32768 | tf_op jit(solution)/shard_map/all_to_all | solution.py:152
  16.0 0.7 convert_element_type.6
  16.6 7.8 %fusion = f32[512,1024]{1,0:T(8,128)} fusion(f32[512,1024]{1,0:T(8,128)} %param.4, f32[512]{0:T(512)S(1)} %convert_element_type.6), kind=kOutput, calls=%fused_computation.5 | convolution fusion | flops 3232235520 | bytes 4196352 | tf_op jit(solution)/shard_map/dot_general | solution.py:34
  24.4 0.0 all-to-all-done.1
  24.4 0.0 copy-start.2
  24.4 0.0 copy-start.1
  24.5 6.0 %all-to-all-start = ((f32[32,16,1024]{2,1,0:T(8,128)}), f32[32,16,1024]{2,1,0:T(8,128)}, u32[]{:S(2)}, u32[]{:S(2)}) async-start(f32[32,16,1024]{2,1,0:T(8,128)} %bitcast.20), calls=%async_computation | async-start | bytes 4194304 | tf_op jit(solution)/shard_map/all_to_all | solution.py:157
  30.4 0.0 all-reduce.3.cloned.1.call-start
  30.5 0.0 copy-done.2
  30.5 0.1 multiply_reduce_fusion.1
  30.6 0.0 copy-done.1
  30.6 3.4 fusion.105
  34.0 1.7 concatenate.7
  35.7 0.5 broadcast.260
  36.2 0.7 reduce.3
  36.9 0.1 mul.84
  37.0 42.2 %all-to-all-done = f32[32,16,1024]{2,1,0:T(8,128)} async-done(((f32[32,16,1024]{2,1,0:T(8,128)}), f32[32,16,1024]{2,1,0:T(8,128)}, u32[]{:S(2)}, u32[]{:S(2)}) %all-to-all-start) | async-done | bytes 2097184 | tf_op jit(solution)/shard_map/all_to_all | solution.py:157
  79.1 6.1 %broadcast_multiply_fusion = (f32[512,1024]{1,0:T(8,128)S(1)}, f32[512,1024]{1,0:T(8,128)S(1)}) fusion(f32[512]{0:T(512)S(1)} %mul.84, f32[512,1024]{1,0:T(8,128)} %bitcast.1, s32[512]{0:T(512)S(1)} %get-tuple-element.27, s32[512]{0:T(512)S(1)} %get-tuple-element.28), kind=kOutput, calls=%fused_computation.42 | convolution fusion | flops 3229614080 | bytes 6297600 | tf_op jit(solution)/shard_map/dot_general | solution.py:34
  85.3 2.1 convolution_dynamic-update-slice_fusion
  87.4 2.0 fusion.8
  89.4 1.8 fusion.11
  91.2 1.7 fusion.14
  92.9 1.5 convolution_dynamic-update-slice_fusion.1
  94.4 1.4 convolution_dynamic-update-slice_fusion.2
  95.8 1.3 convolution_dynamic-update-slice_fusion.3
  97.1 1.2 convolution_dynamic-update-slice_fusion.4
  98.4 0.0 all-reduce.3.cloned.1.call-update
  98.4 0.1 copy.22
  98.5 136.5 %all-reduce.3.cloned.1.call-done = (f32[128,4608]{1,0:T(8,128)}, f32[1032,128]{1,0:T(8,128)}) async-done(((f32[128,4608]{1,0:T(8,128)}, f32[1032,128]{1,0:T(8,128)}), (f32[128,4608]{1,0:T(8,128)}, f32[1032,128]{1,0:T(8,128)})) %all-reduce.3.cloned.1.call-update) | async-done | bytes 2887696 | tf_op jit(solution)/shard_map/psum | solution.py:166
  235.1 1.1 slice.92.atb_ref
  236.2 0.7 slice.93.squares_ref
  236.8 0.0 copy-start
  236.8 1.7 copy-done
  238.5 119.0 %factor_and_solve.1 = (f32[1024,1024]{1,0:T(8,128)}, f32[1024,128]{1,0:T(8,128)S(1)}, f32[8,128]{1,0:T(8,128)S(1)}) custom-call(f32[128,4608]{1,0:T(8,128)S(1)} %copy-done, f32[1024,128]{1,0:T(8,128)S(1)} %slice.92.atb_ref, f32[8,128]{1,0:T(8,128)S(1)} %slice.93.squares_ref), custom_call_target="tpu_custom_call" | custom-call | tf_op jit(solution)/shard_map/factor_and_solve/pallas_call | solution.py:116
  357.5 0.7 multiply_bitcast_fusion
  358.2 2.0 multiply_reduce_fusion
  360.1 40.0 %psum.23 = f32[128]{0:T(128)S(1)} all-reduce(f32[128]{0:T(128)S(1)} %get-tuple-element.25), channel_id=1, replica_groups=mesh['rows'=8,'grp'=4] {'rows','grp'}, use_global_device_ids=true, to_apply=%region_5.6 | all-reduce | flops 128 | bytes 1024 | tf_op jit(solution)/shard_map/psum | solution.py:173
  400.1 0.7 fusion.85
  400.8 0.8 broadcast_multiply_fusion.1
  401.7 0.1 multiply_subtract_fusion
  401.8 0.8 copy.24
  (3 shorter events, 0.0 us)
Async XLA Ops:
  8.6 15.8 %all-to-all-start.1 = ((f32[32,1,16]{2,1,0:T(1,128)}), f32[32,1,16]{2,1,0:T(1,128)S(1)}, u32[]{:S(2)}, u32[]{:S(2)}) async-start(f32[32,1,16]{2,1,0:T(1,128)} %bitcast.2), calls=%async_computation.1 | async-start | bytes 32768 | tf_op jit(solution)/shard_map/all_to_all | solution.py:152
  24.4 6.0 %copy-start.2 = (f32[512,128]{1,0:T(8,128)S(1)}, f32[512,128]{1,0:T(8,128)}, u32[]{:S(2)}) copy-start(f32[512,128]{1,0:T(8,128)} %param.7) | copy-start | bytes 786436
  24.4 6.1 %copy-start.1 = (f32[512,1024]{1,0:T(8,128)S(1)}, f32[512,1024]{1,0:T(8,128)}, u32[]{:S(2)}) copy-start(f32[512,1024]{1,0:T(8,128)} %param.4) | copy-start | bytes 6291460
  24.5 54.7 %all-to-all-start = ((f32[32,16,1024]{2,1,0:T(8,128)}), f32[32,16,1024]{2,1,0:T(8,128)}, u32[]{:S(2)}, u32[]{:S(2)}) async-start(f32[32,16,1024]{2,1,0:T(8,128)} %bitcast.20), calls=%async_computation | async-start | bytes 4194304 | tf_op jit(solution)/shard_map/all_to_all | solution.py:157
  30.4 204.6 %all-reduce.3.cloned.1.call-start = ((), (), s32[]{:S(2)}) async-start(), calls=%async_computation.2 | async-start | bytes 5775360 | tf_op jit(solution)/shard_map/psum | solution.py:166
  236.8 1.7 copy-start
Sparse Core Ops, SparseCore 0:
  98.5 136.5 all-reduce.2

commit v2 on v1

--- a/solution.py
+++ b/solution.py
@@ -67,11 +67,11 @@
     tiles = n // TILE
     offset = 0
     for i in range(tiles):
-        width = n - i * TILE
-        work[i * TILE:(i + 1) * TILE, i * TILE:n] = packed_ref[:, offset:offset + width]
+        for j in range(i, tiles):
+            work[i * TILE:(i + 1) * TILE, j * TILE:(j + 1) * TILE] = packed_ref[offset:offset + TILE, :]
+            offset += TILE
         if i:
             work[i * TILE:(i + 1) * TILE, :i * TILE] = jnp.zeros((TILE, i * TILE), jnp.float32)
-        offset += width
     work[:, n:] = atb_ref[...]
     width = work.shape[1]
 
@@ -138,18 +138,25 @@
     piece = row_count // devices
 
     atb_part = dot_tt(mat, rhs)
-    squares_part = jnp.sum(rhs * rhs, axis=0, keepdims=True)
-    squares_part = jnp.concatenate(
-        [squares_part, jnp.zeros((SUB - 1, rhs.shape[1]), jnp.float32)], axis=0
-    )
-    early = lax.psum(jnp.concatenate([atb_part, squares_part], axis=0), AXES)
-    atb, squares = early[:n], early[n:]
+    atb = lax.psum(atb_part, AXES)
 
     local_rows = lax.iota(jnp.int32, row_count)
     hits = jnp.sum(
         ((picks % row_count)[:, None] == local_rows[None, :]).astype(jnp.float32), axis=0
     ) * (1.0 / samples)
-    hits = lax.all_to_all(hits.reshape(devices, piece), AXES, 0, 0, tiled=True)
+    squares_part = jnp.sum(rhs * rhs, axis=0, keepdims=True)
+    small = jnp.concatenate(
+        [
+            jnp.broadcast_to(squares_part, (devices, rhs.shape[1])),
+            hits.reshape(devices, piece),
+        ],
+        axis=1,
+    )
+    small = lax.all_to_all(small, AXES, 0, 0, tiled=True)
+    hits = small[:, rhs.shape[1]:]
+    squares = jnp.broadcast_to(
+        jnp.sum(small[:, :rhs.shape[1]], axis=0, keepdims=True), (SUB, rhs.shape[1])
+    )
 
     mixed = mat * signs.astype(jnp.float32)[:, None]
     mixed = dot_nn(walsh_table(row_count), mixed)
@@ -163,14 +170,21 @@
     strips = [
         dot_tt(weighted[:, at:at + TILE], turned[:, at:]) for at in range(0, n, TILE)
     ]
-    packed = lax.psum(jnp.concatenate(strips, axis=1), AXES)
+    tiles = [
+        strip[:, at:at + TILE] for strip in strips for at in range(0, strip.shape[1], TILE)
+    ]
+    packed = lax.psum(jnp.concatenate(tiles, axis=0), AXES)
 
     tri, direction, alpha = factor_and_solve(packed, atb, squares)
     alpha = alpha[0]
     beta = jnp.sqrt(squares[0])
     image = dot_nn(mat, direction)
     pushed = image - alpha / beta * rhs
-    gamma_sq = lax.psum(jnp.sum(pushed * pushed, axis=0), AXES)
+    gamma_part = jnp.sum(pushed * pushed, axis=0, keepdims=True)
+    gamma_parts = lax.all_to_all(
+        jnp.broadcast_to(gamma_part, (devices, rhs.shape[1])), AXES, 0, 0, tiled=True
+    )
+    gamma_sq = jnp.sum(gamma_parts, axis=0)
     coef = beta * alpha / (alpha * alpha + gamma_sq)
     return (tri, direction * coef, rhs - image * coef)
 

time: 410 us -> 397 us (0.968)
  blocking collectives: 40 us -> 10.4 us
  local copies, waits for them, and re-layouts: 7.34 us -> 26.7 us
    psum x1 -> x0, blocking collectives: 40 us -> none  [shards(): gamma_sq = lax.psum(jnp.sum(pushed * pushed, axis=0), AXES)]
    unnamed x8 -> x46, local copies, waits for them, and re-layouts: 2.64 us -> 25.9 us
    all_to_all x0 -> x1, blocking collectives: none -> 10.4 us  [shards(): lax.all_to_all(jnp.broadcast_to(gamma_part, (devices, rhs.shape[1])), AXE...]
  transfers between devices with their start and end apart: 3 -> 3, of which waited for: 2 -> 2; matrix products, arithmetic and copies ran while one was open for 4% -> 3% of each run, Pallas kernels for 0% -> 0%
where the time goes in v2:
time: 397 us
  waiting for transfers between devices  181 us (46%)
  Pallas kernels  119 us (30%)
  matrix products  28.3 us (7%)
  local copies, waits for them, and re-layouts  26.7 us (7%)
  between operations  14.2 us (4%)
  starting transfers between devices  13.5 us (3%)
  blocking collectives  10.4 us (3%)
    psum x1, waiting for transfers between devices, shards(): packed = lax.psum(jnp.concatenate(tiles, axis=0), AXES)  137 us
    pallas_call x1, Pallas kernels, factor_and_solve(): pl.pallas_call(factor_kernel, out_shape=(jax.ShapeDtypeStruct((n, n), jnp...  119 us
    all_to_all x1, waiting for transfers between devices, shards(): turned = lax.all_to_all(mixed, AXES, 0, 0, tiled=True)  44.1 us
    unnamed x46, local copies, waits for them, and re-layouts  25.9 us
    dot_general x3, matrix products, dot_nn(): lax.dot_general(a, b, (((1,), (0,)), ((), ())), precision=exact_mode, pre...  15.9 us
    dot_general x9, matrix products, dot_tt(): lax.dot_general(a, b, (((0,), (0,)), ((), ())), precision=exact_mode, pre...  12.4 us
    all_to_all x1, blocking collectives, shards(): lax.all_to_all(jnp.broadcast_to(gamma_part, (devices, rhs.shape[1])), AXE...  10.4 us
  transfers between devices with their start and end apart: 3, of which 2 were waited for; matrix products, arithmetic and copies ran while one was open for 3% of the time, Pallas kernels for 0%

profile of v2, /device:TPU:0, one launch (start us, length us, event | category | flops | bytes accessed | tf_op | source)
XLA Modules:
  0.0 396.7 jit_solution(1145848020217883029)
XLA Ops:
  7.2 0.7 and_select_fusion
  8.0 1.0 multiply_reduce_fusion.1
  9.1 0.6 all_to_all.23
  9.7 7.3 %all-to-all-start.1 = ((f32[32,1,144]{2,1,0:T(1,128)}), f32[32,1,144]{2,1,0:T(1,128)S(1)}, u32[]{:S(2)}, u32[]{:S(2)}) async-start(f32[32,1,144]{2,1,0:T(1,128)} %all_to_all.23), calls=%async_computation.1 | async-start | bytes 65536 | tf_op jit(solution)/shard_map/all_to_all | solution.py:155
  17.0 0.7 convert_element_type.6
  17.7 7.8 %fusion = f32[512,1024]{1,0:T(8,128)} fusion(f32[512,1024]{1,0:T(8,128)} %param.4, f32[512]{0:T(512)S(1)} %convert_element_type.6), kind=kOutput, calls=%fused_computation.5 | convolution fusion | flops 3232235520 | bytes 4196352 | tf_op jit(solution)/shard_map/dot_general | solution.py:34
  25.5 6.0 %all-to-all-start = ((f32[32,16,1024]{2,1,0:T(8,128)}), f32[32,16,1024]{2,1,0:T(8,128)}, u32[]{:S(2)}, u32[]{:S(2)}) async-start(f32[32,16,1024]{2,1,0:T(8,128)} %bitcast.34), calls=%async_computation | async-start | bytes 4194304 | tf_op jit(solution)/shard_map/all_to_all | solution.py:164
  31.8 4.2 %fusion.102 = f32[1024,128]{1,0:T(8,128)} fusion(f32[512,1024]{1,0:T(8,128)S(1)} %copy-done.2, f32[512,128]{1,0:T(8,128)S(1)} %copy-done.3), kind=kOutput, calls=%fused_computation.170 | convolution fusion | flops 805306368 | bytes 2883584 | tf_op jit(solution)/shard_map/dot_general | solution.py:29
  36.1 44.1 %all-to-all-done = f32[32,16,1024]{2,1,0:T(8,128)} async-done(((f32[32,16,1024]{2,1,0:T(8,128)}), f32[32,16,1024]{2,1,0:T(8,128)}, u32[]{:S(2)}, u32[]{:S(2)}) %all-to-all-start) | async-done | bytes 2097184 | tf_op jit(solution)/shard_map/all_to_all | solution.py:164
  80.2 6.1 %broadcast_multiply_fusion = (f32[512,1024]{1,0:T(8,128)S(1)}, f32[512,1024]{1,0:T(8,128)S(1)}) fusion(f32[512]{0:T(512)S(1)} %mul.76, f32[512,1024]{1,0:T(8,128)} %bitcast.1, s32[512]{0:T(512)S(1)} %get-tuple-element.30, s32[512]{0:T(512)S(1)} %get-tuple-element.31), kind=kOutput, calls=%fused_computation.36 | convolution fusion | flops 3229614080 | bytes 6297600 | tf_op jit(solution)/shard_map/dot_general | solution.py:34
  86.4 1.3 fusion.72
  87.7 1.2 fusion.2
  88.9 1.1 fusion.4
  90.0 1.0 fusion.6
  91.0 1.0 fusion.21
  92.0 0.7 fusion.37
  93.4 0.6 constant_dynamic-update-slice_fusion.34
  94.0 0.6 constant_dynamic-update-slice_fusion.33
  94.7 0.6 constant_dynamic-update-slice_fusion.32
  95.3 0.6 constant_dynamic-update-slice_fusion.31
  95.9 0.6 constant_dynamic-update-slice_fusion.30
  96.6 0.6 constant_dynamic-update-slice_fusion.29
  97.2 0.6 constant_dynamic-update-slice_fusion.28
  97.9 0.6 constant_dynamic-update-slice_fusion.27
  98.5 0.6 constant_dynamic-update-slice_fusion.26
  99.1 0.6 constant_dynamic-update-slice_fusion.25
  99.8 0.6 constant_dynamic-update-slice_fusion.24
  100.4 0.6 constant_dynamic-update-slice_fusion.23
  101.0 0.6 constant_dynamic-update-slice_fusion.22
  101.7 0.6 constant_dynamic-update-slice_fusion.21
  104.8 0.6 constant_dynamic-update-slice_fusion.16
  106.1 0.6 constant_dynamic-update-slice_fusion.14
  107.4 0.6 constant_dynamic-update-slice_fusion.12
  108.6 0.6 constant_dynamic-update-slice_fusion.10
  109.9 0.6 constant_dynamic-update-slice_fusion.8
  110.5 0.6 constant_dynamic-update-slice_fusion.7
  111.2 0.6 constant_dynamic-update-slice_fusion.6
  111.8 0.6 constant_dynamic-update-slice_fusion.5
  114.4 0.6 constant_dynamic-update-slice_fusion.1
  115.6 1.2 convolution_dynamic-update-slice_fusion
  117.1 137.1 %all-reduce.3.cloned.1.call-done = (f32[4608,128]{1,0:T(8,128)}, f32[1024,128]{1,0:T(8,128)}) async-done(((f32[4608,128]{1,0:T(8,128)}, f32[1024,128]{1,0:T(8,128)}), (f32[4608,128]{1,0:T(8,128)}, f32[1024,128]{1,0:T(8,128)})) %all-reduce.3.cloned.1.call-update) | async-done | bytes 2883600 | tf_op jit(solution)/shard_map/psum | solution.py:176
  254.2 1.7 copy-done
  255.8 1.0 copy-done.1
  256.9 118.8 %factor_and_solve.1 = (f32[1024,1024]{1,0:T(8,128)}, f32[1024,128]{1,0:T(8,128)S(1)}, f32[8,128]{1,0:T(8,128)S(1)}) custom-call(f32[4608,128]{1,0:T(8,128)S(1)} %copy-done, f32[1024,128]{1,0:T(8,128)S(1)} %copy-done.1, f32[8,128]{1,0:T(8,128)S(1)} %broadcast_in_dim.25.squares_ref), custom_call_target="tpu_custom_call" | custom-call | tf_op jit(solution)/shard_map/factor_and_solve/pallas_call | solution.py:116
  375.7 2.0 multiply_reduce_fusion
  377.7 10.4 %all_to_all.30 = f32[32,1,128]{2,1,0:T(1,128)S(1)} all-to-all(f32[32,1,128]{2,1,0:T(1,128)S(1)} %broadcast_in_dim.26), channel_id=1, replica_groups=mesh['rows'=8,'grp'=4] {'rows','grp'}, dimensions={0} | all-to-all | bytes 32768 | tf_op jit(solution)/shard_map/all_to_all | solution.py:184
  388.1 0.8 broadcast_multiply_fusion.1
  389.0 0.8 copy.22
  (39 shorter events, 9.1 us)
Async XLA Ops:
  9.7 15.8 %all-to-all-start.1 = ((f32[32,1,144]{2,1,0:T(1,128)}), f32[32,1,144]{2,1,0:T(1,128)S(1)}, u32[]{:S(2)}, u32[]{:S(2)}) async-start(f32[32,1,144]{2,1,0:T(1,128)} %all_to_all.23), calls=%async_computation.1 | async-start | bytes 65536 | tf_op jit(solution)/shard_map/all_to_all | solution.py:155
  25.5 6.2 %copy-start.2 = (f32[512,1024]{1,0:T(8,128)S(1)}, f32[512,1024]{1,0:T(8,128)}, u32[]{:S(2)}) copy-start(f32[512,1024]{1,0:T(8,128)} %param.4) | copy-start | bytes 6291460
  25.5 6.2 %copy-start.3 = (f32[512,128]{1,0:T(8,128)S(1)}, f32[512,128]{1,0:T(8,128)}, u32[]{:S(2)}) copy-start(f32[512,128]{1,0:T(8,128)} %param.7) | copy-start | bytes 786436
  25.5 54.7 %all-to-all-start = ((f32[32,16,1024]{2,1,0:T(8,128)}), f32[32,16,1024]{2,1,0:T(8,128)}, u32[]{:S(2)}, u32[]{:S(2)}) async-start(f32[32,16,1024]{2,1,0:T(8,128)} %bitcast.34), calls=%async_computation | async-start | bytes 4194304 | tf_op jit(solution)/shard_map/all_to_all | solution.py:164
  31.5 222.7 %all-reduce.3.cloned.1.call-start = ((), (), s32[]{:S(2)}) async-start(), calls=%async_computation.3 | async-start | bytes 5767168 | tf_op jit(solution)/shard_map/psum | solution.py:176
  254.2 1.7 copy-start
  255.8 1.0 copy-start.1
Sparse Core Ops, SparseCore 0:
  117.0 137.1 all-reduce.2
